TPU v7x, 512 devices: a whole 4x4x16 slice. The times are simulated.
512 devices in a mesh: feat: 64 (over x, z_hi, y, core), tok: 8 (over z_lo).
Axes of the slice: x: 4, y: 4, z: 16 (z_hi: 2, z_lo: 8; z = z_hi * 8 + z_lo), core: 2. Of those that a mesh axis runs over, the one named last changes fastest.
Arguments:
- features: bfloat16 [1024, 131072], P('tok', 'feat'), may hold values from -6 to 6
- signs: int32 [131072], P('feat'), may hold values from -1 to 1, as said below
- columns: int32 [1024], replicated, may hold values from 0 to 131071, as said below
- labels: int32 [1024, 1], P('tok'), may hold values from 0 to 31; in each aligned block of 128 rows (0 to 127, 128 to 255, ...) at most 8 rows name the same one
Outputs:
- gram: float32 [32, 1024, 1024], P('tok', 'feat')
Inputs may be any that keep to these rules, and one draw needn't show every extreme that they name: `signs`: every entry is -1 or 1. `columns`: the 1024 indices are distinct. `labels`: among the rows of one device no concept appears more than 8 times.
All inputs are finite; a program needn't handle non-finite values.
Results may differ from a plain program's by a relative error of at most 0.004.
Values may be sent and summed in bfloat16 or wider, within the bound.
A program may use at most 64 MiB of HBM per device.

v0:
```python
import math

import jax
import jax.numpy as jnp
from jax import lax
from jax.sharding import PartitionSpec as P

C = 32


def from_partner(array, axis, distance):
    return lax.ppermute(array, axis, [(i, i ^ 1 << distance) for i in range(lax.axis_size(axis))])


def bit_parity(number, bit_count):
    total = jnp.zeros_like(number)
    for position in range(bit_count):
        total = total ^ number >> position & 1
    return total


def sylvester(order, dtype):
    index = lax.iota(jnp.int32, order)
    parity = bit_parity(index[:, None] & index[None, :], order.bit_length())
    return (1 - 2 * parity).astype(dtype)


def body(features, signs, columns, labels):
    rows, width = features.shape
    feat_count = lax.axis_size("feat")
    feat_index = lax.axis_index("feat")
    tok_count = lax.axis_size("tok")
    kept = columns.shape[0]
    shard_cols = kept // feat_count
    flat_labels = labels[:, 0]
    signed = features * signs.astype(jnp.bfloat16)[None, :]
    transformed = jnp.dot(
        signed, sylvester(width, jnp.bfloat16), preferred_element_type=jnp.float32
    )
    local_col = columns % width
    owner = columns // width
    sections = feat_count.bit_length() - 1
    for section in range(sections):
        partner = from_partner(transformed, "feat", section)
        upper = feat_index >> section & 1 == 1
        transformed = jnp.where(upper, partner - transformed, transformed + partner)
    picked = jnp.take(transformed, local_col, axis=1)
    owned = (owner == feat_index)[None, :]
    combined = lax.psum(jnp.where(owned, picked, 0.0), "feat")
    sketch = (combined * (1.0 / math.sqrt(width * feat_count))).astype(jnp.bfloat16)
    factor = C / (rows * tok_count)
    own_rows = lax.dynamic_slice_in_dim(sketch, feat_index * shard_cols, shard_cols, 1)
    wanted = lax.iota(jnp.int32, C // tok_count * lax.axis_size("tok"))
    onehot = (flat_labels[:, None] == wanted[None, :]).astype(jnp.bfloat16)
    weighted = (onehot[:, :, None] * own_rows[:, None, :]).reshape(
        rows, C // tok_count * lax.axis_size("tok") * shard_cols
    )
    partial_gram = jnp.einsum("rm,rk->mk", weighted, sketch, preferred_element_type=jnp.float32)
    return lax.psum_scatter(
        partial_gram.reshape(C // tok_count * lax.axis_size("tok"), shard_cols, kept) * factor,
        "tok",
        scatter_dimension=0,
        tiled=True,
    )


def solution(mesh):
    in_specs = (P("tok", "feat"), P("feat"), P(), P("tok", None))
    out_specs = P("tok", "feat", None)
    return jax.shard_map(body, mesh=mesh, in_specs=in_specs, out_specs=out_specs, check_vma=False)
```

profile of v0, /device:TPU:1, one launch (start us, length us, event | category | flops | bytes accessed | tf_op | source)
XLA Modules:
  0.0 1405.8 jit_solution(11742431662747528848)
XLA Ops:
  6.5 0.0 all-reduce.2.cloned.1.call-start
  6.5 0.7 convert_element_type.17
  7.2 23.5 %fusion = f32[128,2048]{1,0:T(8,128)S(1)} fusion(bf16[128,2048]{1,0:T(8,128)(2,1)} %param.4, bf16[2048]{0:T(1024)(128)(2,1)S(1)} %convert_element_type.17), kind=kOutput, calls=%fused_computation.2 | convolution fusion | flops 1237581824 | bytes 1576960 | tf_op jit(solution)/shard_map/dot_general | solution.py:37
  30.8 8.8 collective-permute-start
  39.6 2.3 collective-permute-done
  41.8 0.1 add_select_fusion.5
  42.0 1.9 collective-permute-start.1
  43.9 24.3 %collective-permute-done.1 = f32[128,2048]{1,0:T(8,128)S(1)} collective-permute-done((f32[128,2048]{1,0:T(8,128)S(1)}, f32[128,2048]{1,0:T(8,128)S(1)}, u32[]{:S(2)}, u32[]{:S(2)}) %collective-permute-start.1) | collective-permute-done | bytes 1048608 | tf_op jit(solution)/shard_map/ppermute | solution.py:12
  68.2 0.1 add_select_fusion.4
  68.4 1.9 collective-permute-start.2
  70.3 24.9 %collective-permute-done.2 = f32[128,2048]{1,0:T(8,128)S(1)} collective-permute-done((f32[128,2048]{1,0:T(8,128)S(1)}, f32[128,2048]{1,0:T(8,128)S(1)}, u32[]{:S(2)}, u32[]{:S(2)}) %collective-permute-start.2) | collective-permute-done | bytes 1048608 | tf_op jit(solution)/shard_map/ppermute | solution.py:12
  95.3 0.1 add_select_fusion.3
  95.4 10.1 collective-permute-start.3
  105.5 57.7 %collective-permute-done.3 = f32[128,2048]{1,0:T(8,128)S(1)} collective-permute-done((f32[128,2048]{1,0:T(8,128)S(1)}, f32[128,2048]{1,0:T(8,128)S(1)}, u32[]{:S(2)}, u32[]{:S(2)}) %collective-permute-start.3) | collective-permute-done | bytes 1048608 | tf_op jit(solution)/shard_map/ppermute | solution.py:12
  163.2 0.1 add_select_fusion.2
  163.3 0.0 copy-start
  163.3 1.9 collective-permute-start.4
  165.3 22.8 %collective-permute-done.4 = f32[128,2048]{1,0:T(8,128)S(1)} collective-permute-done((f32[128,2048]{1,0:T(8,128)S(1)}, f32[128,2048]{1,0:T(8,128)S(1)}, u32[]{:S(2)}, u32[]{:S(2)}) %collective-permute-start.4) | collective-permute-done | bytes 1048608 | tf_op jit(solution)/shard_map/ppermute | solution.py:12
  188.0 0.1 add_select_fusion.1
  188.2 1.9 collective-permute-start.5
  190.1 0.0 copy-done
  190.1 23.3 %collective-permute-done.5 = f32[128,2048]{1,0:T(8,128)S(1)} collective-permute-done((f32[128,2048]{1,0:T(8,128)S(1)}, f32[128,2048]{1,0:T(8,128)S(1)}, u32[]{:S(2)}, u32[]{:S(2)}) %collective-permute-start.5) | collective-permute-done | bytes 1048608 | tf_op jit(solution)/shard_map/ppermute | solution.py:12
  213.4 0.1 add_select_fusion
  213.6 0.3 copy.5
  213.9 2.8 gather_fusion
  216.7 0.0 copy-start.1
  216.8 0.2 copy.6
  217.0 0.8 select_bitcast_fusion
  217.8 0.0 all-reduce.2.cloned.1.call-update
  217.8 0.0 reduce-scatter.2.cloned.1.call-start
  217.9 0.0 copy-done.1
  217.9 1109.5 %all-reduce.2.cloned.1.call-done = f32[128,1024]{1,0:T(8,128)} async-done(((f32[128,1024]{1,0:T(8,128)}), f32[128,1024]{1,0:T(8,128)}) %all-reduce.2.cloned.1.call-update) | async-done | bytes 524304 | tf_op jit(solution)/shard_map/psum | solution.py:49
  1327.4 1.1 multiply_convert_fusion
  1328.5 0.1 constant_dynamic-slice_fusion
  1328.6 0.1 copy.7
  1328.7 1.8 convolution_multiply_fusion
  1330.5 0.0 reduce-scatter.2.cloned.1.call-update
  1330.5 68.5 %reduce-scatter.2.cloned.1.call-done = f32[4,16,1024]{2,1,0:T(8,128)} async-done(((f32[32,16,1024]{2,1,0:T(8,128)}), f32[4,16,1024]{2,1,0:T(8,128)}) %reduce-scatter.2.cloned.1.call-update) | async-done | bytes 262160 | tf_op jit(solution)/shard_map/reduce_scatter | solution.py:59
  (3 shorter events, 0.0 us)
Async XLA Ops:
  6.5 1320.9 %all-reduce.2.cloned.1.call-start = ((), (), s32[]{:S(2)}) async-start(), calls=%async_computation.1 | async-start | bytes 1048576 | tf_op jit(solution)/shard_map/psum | solution.py:49
  30.8 11.1 collective-permute-start
  42.0 26.3 %collective-permute-start.1 = (f32[128,2048]{1,0:T(8,128)S(1)}, f32[128,2048]{1,0:T(8,128)S(1)}, u32[]{:S(2)}, u32[]{:S(2)}) collective-permute-start(f32[128,2048]{1,0:T(8,128)S(1)} %add_select_fusion.5), channel_id=1, source_target_pairs={{0,16},{8,24},{16,0},{24,8},{32,48},{40,56},{48,32},{56,40},{64,80... | collective-permute-start | bytes 3145736 | tf_op jit(solution)/shard_map/ppermute | solution.py:12
  68.4 26.8 %collective-permute-start.2 = (f32[128,2048]{1,0:T(8,128)S(1)}, f32[128,2048]{1,0:T(8,128)S(1)}, u32[]{:S(2)}, u32[]{:S(2)}) collective-permute-start(f32[128,2048]{1,0:T(8,128)S(1)} %add_select_fusion.4), channel_id=1, source_target_pairs={{0,32},{8,40},{16,48},{24,56},{32,0},{40,8},{48,16},{56,24},{64,96... | collective-permute-start | bytes 3145736 | tf_op jit(solution)/shard_map/ppermute | solution.py:12
  95.4 67.8 %collective-permute-start.3 = (f32[128,2048]{1,0:T(8,128)S(1)}, f32[128,2048]{1,0:T(8,128)S(1)}, u32[]{:S(2)}, u32[]{:S(2)}) collective-permute-start(f32[128,2048]{1,0:T(8,128)S(1)} %add_select_fusion.3), channel_id=1, source_target_pairs={{0,64},{8,72},{16,80},{24,88},{32,96},{40,104},{48,112},{56,120},{... | collective-permute-start | bytes 3145736 | tf_op jit(solution)/shard_map/ppermute | solution.py:12
  163.3 26.8 %copy-start = (s32[1024]{0:T(1024)S(1)}, s32[1024]{0:T(1024)}, u32[]{:S(2)}) copy-start(s32[1024]{0:T(1024)} %param.6) | copy-start | bytes 12292
  163.3 24.7 %collective-permute-start.4 = (f32[128,2048]{1,0:T(8,128)S(1)}, f32[128,2048]{1,0:T(8,128)S(1)}, u32[]{:S(2)}, u32[]{:S(2)}) collective-permute-start(f32[128,2048]{1,0:T(8,128)S(1)} %add_select_fusion.2), channel_id=1, source_target_pairs={{0,128},{8,136},{16,144},{24,152},{32,160},{40,168},{48,176},{56,1... | collective-permute-start | bytes 3145736 | tf_op jit(solution)/shard_map/ppermute | solution.py:12
  188.2 25.3 %collective-permute-start.5 = (f32[128,2048]{1,0:T(8,128)S(1)}, f32[128,2048]{1,0:T(8,128)S(1)}, u32[]{:S(2)}, u32[]{:S(2)}) collective-permute-start(f32[128,2048]{1,0:T(8,128)S(1)} %add_select_fusion.1), channel_id=1, source_target_pairs={{0,256},{8,264},{16,272},{24,280},{32,288},{40,296},{48,304},{56,3... | collective-permute-start | bytes 3145736 | tf_op jit(solution)/shard_map/ppermute | solution.py:12
  216.7 1.1 copy-start.1
  217.8 1181.1 %reduce-scatter.2.cloned.1.call-start = ((), (), s32[]{:S(2)}) async-start(), calls=%async_computation.2 | async-start | bytes 2359296 | tf_op jit(solution)/shard_map/reduce_scatter | solution.py:59
Sparse Core Ops, SparseCore 0:
  217.9 1109.4 all-reduce.1
  1330.6 68.2 reduce-scatter.1
where the time goes:
time: 1410 us
  waiting for transfers between devices  1330 us (94%)
  starting transfers between devices  26.6 us (2%)
  matrix products  25.3 us (2%)
    psum x1, waiting for transfers between devices, body(): combined = lax.psum(jnp.where(owned, picked, 0.0), 'feat')  1110 us
    ppermute x6, waiting for transfers between devices, from_partner(): lax.ppermute(array, axis, [(i, i ^ 1 << distance) for i in range(lax.axis...  155 us
    reduce_scatter x1, waiting for transfers between devices, body(): lax.psum_scatter(partial_gram.reshape(C // tok_count * lax.axis_size('tok...  68.5 us
  transfers between devices with their start and end apart: 8, of which 8 were waited for; matrix products, arithmetic and copies ran while one was open for 0% of the time, Pallas kernels for 0%

commit v1 on v0

v1 whole, which is shorter than its diff:
```python
import math

import jax
import jax.numpy as jnp
from jax import lax
from jax.experimental import pallas as pl
from jax.experimental.pallas import tpu as pltpu
from jax.sharding import PartitionSpec as P

C = 32
MESH = pl.DeviceIdType.MESH
NX, NH, NY, NC, NG = 4, 2, 4, 2, 8
NXY = NX * NY
NZ = NH * NG


def kernel(x_ref, sg_ref, col_ref, lab_ref, out_ref, xs, s, y, r1, r2, fold, r3, g,
           send1, recv1, send2, recv2, send3, recv3, send4, recv4, send5, recv5):
    f = lax.axis_index("feat")
    tok = lax.axis_index("tok")
    core = f % NC
    py = f // NC % NY
    zh = f // (NC * NY) % NH
    px = f // (NC * NY * NH)
    xy = px * NY + py
    plane = zh * NG + tok

    def feat_of(qx, qh, qy, qc):
        return ((qx * NH + qh) * NY + qy) * NC + qc

    sibling = {"feat": feat_of(px, zh, py, 1 - core), "tok": tok}

    def xy_at(d):
        return (px + d // NY) % NX, (py + d % NY) % NY

    def xy_device(d):
        qx, qy = xy_at(d)
        return {"feat": feat_of(qx, zh, qy, core), "tok": tok}

    def z_device(d):
        other = (plane + d) % NZ
        return {"feat": feat_of(px, other // NG, py, core), "tok": other % NG}

    barrier = pltpu.get_barrier_semaphore()
    pl.semaphore_signal(barrier, inc=1, device_id=sibling, device_id_type=MESH)
    for d in range(1, NXY):
        pl.semaphore_signal(barrier, inc=1, device_id=xy_device(d), device_id_type=MESH)
    for d in range(1, NZ):
        pl.semaphore_signal(barrier, inc=1, device_id=z_device(d), device_id_type=MESH)

    xs[...] = x_ref[...] * sg_ref[...].astype(jnp.float32).astype(jnp.bfloat16)
    lane = lax.broadcasted_iota(jnp.int32, (128, 128), 1)

    def chunk(i):
        c = jnp.broadcast_to(col_ref[pl.ds(i, 1), :], (128, 128)).T
        v = (c & lane) ^ (c >> 11 & f)
        v = v ^ v >> 4
        v = v ^ v >> 2
        v = v ^ v >> 1
        parts = [(1 - 2 * (v & 1)).astype(jnp.float32).astype(jnp.bfloat16)]
        for bit in range(4):
            flip = (1 - 2 * (c >> 7 + bit & 1)).astype(jnp.float32).astype(jnp.bfloat16)
            parts = parts + [part * flip for part in parts]
        for block in range(16):
            s[:, 128 * block:128 * block + 128] = parts[block]
        found = lax.dot_general(s[...], xs[...], (((1,), (1,)), ((), ())), preferred_element_type=jnp.float32)
        y[pl.ds(4 * i, 4)] = found.reshape(4, 32, 128)

    @pl.loop(0, 4)
    def _(n):
        chunk(4 * (1 - core) + n)

    pl.semaphore_wait(barrier, 1 + (NXY - 1) + (NZ - 1))
    pair = pltpu.make_async_remote_copy(
        src_ref=y.at[pl.ds(NXY * (1 - core), NXY)], dst_ref=r1, send_sem=send1, recv_sem=recv1,
        device_id=sibling, device_id_type=MESH)
    pair.start()

    @pl.loop(0, 4)
    def _(n):
        chunk(4 * core + n)

    row = jnp.broadcast_to(lab_ref[...], (128, 128))
    col = row.T
    above = lax.broadcasted_iota(jnp.int32, (128, 128), 0)
    earlier = jnp.where((row == col) & (lane < above), 1.0, 0.0)
    rank = jnp.sum(earlier, axis=1, keepdims=True)
    slot = col.astype(jnp.float32) * 8.0 + rank
    within = (lane % 32).astype(jnp.float32)
    spread = jnp.concatenate(
        [jnp.where(slot == within + 32.0 * q, 1.0, 0.0).astype(jnp.bfloat16) for q in range(NG)], axis=1)

    pair.wait_recv()
    out2 = []
    for d in range(1, NXY):
        qx, qy = xy_at(d)
        there = qx * NY + qy
        mine = NXY * core + there
        y[mine] = y[mine] + r1[there]
        copy = pltpu.make_async_remote_copy(
            src_ref=y.at[mine], dst_ref=r2.at[d - 1], send_sem=send2.at[d - 1], recv_sem=recv2.at[d - 1],
            device_id=xy_device(d), device_id_type=MESH)
        copy.start()
        out2.append(copy)
    total = y[NXY * core + xy] + r1[xy]
    for d in range(1, NXY):
        out2[d - 1].wait_recv()
        total = total + r2[d - 1]

    hi = total.astype(jnp.bfloat16)
    rest = total - hi.astype(jnp.float32)
    mid = rest.astype(jnp.bfloat16)
    low = (rest - mid.astype(jnp.float32)).astype(jnp.bfloat16)
    picked = jnp.dot(jnp.concatenate([hi, mid, low], axis=0), spread, preferred_element_type=jnp.float32)
    picked = picked[0:32] + picked[32:64] + picked[64:96]
    quarter = lax.broadcasted_iota(jnp.int32, (8, 128), 1) // 32
    for q in range(NG):
        tile = picked[0:8, 128 * q:128 * q + 128]
        for k in range(1, 4):
            tile = jnp.where(quarter == k, picked[8 * k:8 * k + 8, 128 * q:128 * q + 128], tile)
        fold[q] = tile
    out3 = []
    for d in range(1, NZ):
        copy = pltpu.make_async_remote_copy(
            src_ref=fold.at[(plane + d) % NG], dst_ref=r3.at[d - 1], send_sem=send3.at[d - 1],
            recv_sem=recv3.at[d - 1], device_id=z_device(d), device_id_type=MESH)
        copy.start()
        out3.append(copy)
    for d in range(1, NZ):
        out3[d - 1].wait_recv()
    scale = 1.0 / math.sqrt(131072)
    tiles = []
    for d in range(NG):
        first = fold[plane % NG] if d == 0 else r3[d - 1]
        tiles.append((first + r3[d + NG - 1]) * scale)
    rows = []
    for k in range(4):
        halves = []
        for h in range(2):
            piece = None
            for j in range(4):
                moved = tiles[4 * h + j]
                if j != k:
                    moved = pltpu.roll(moved, (j - k) % 4 * 32, 1)
                piece = moved if piece is None else jnp.where(quarter == j, moved, piece)
            halves.append(piece)
        rows.append(jnp.concatenate(halves, axis=1))
    mine = NXY * core + xy
    g[mine] = jnp.concatenate(rows, axis=0).astype(jnp.bfloat16)

    out5 = []

    def forward(d, block):
        copy = pltpu.make_async_remote_copy(
            src_ref=g.at[block], dst_ref=g.at[block], send_sem=send5.at[d], recv_sem=recv5.at[d],
            device_id=sibling, device_id_type=MESH)
        copy.start()
        out5.append(copy)

    out4 = []
    for d in range(1, NXY):
        copy = pltpu.make_async_remote_copy(
            src_ref=g.at[mine], dst_ref=g.at[mine], send_sem=send4.at[d - 1], recv_sem=recv4.at[d - 1],
            device_id=xy_device(d), device_id_type=MESH)
        copy.start()
        out4.append(copy)
    forward(0, mine)
    for d in range(1, NXY):
        out4[d - 1].wait_recv()
        came = (px - d // NY + NX) % NX * NY + (py - d % NY + NY) % NY
        forward(d, NXY * core + came)
    for copy in out5:
        copy.wait_recv()

    own = g[f // 2, pl.ds(pl.multiple_of(f % 2 * 16, 16), 16), :]
    concept = lax.broadcasted_iota(jnp.int32, (16, 256), 1) % 32 // 8
    left = jnp.concatenate([jnp.where(concept == k, own, jnp.zeros_like(own)) for k in range(4)], axis=0)
    gram = lax.dot_general(left, g[...].reshape(1024, 256), (((1,), (1,)), ((), ())),
                           preferred_element_type=jnp.float32)
    out_ref[...] = (gram * (C / 1024)).reshape(4, 16, 1024)
    pair.wait_send()
    for copy in out2 + out3 + out4 + out5:
        copy.wait_send()


def body(features, signs, columns, labels):
    vmem = pl.BlockSpec(memory_space=pltpu.VMEM)
    dma = pltpu.SemaphoreType.DMA
    return pl.pallas_call(
        kernel,
        out_shape=jax.ShapeDtypeStruct((4, 16, 1024), jnp.float32),
        in_specs=[vmem] * 4,
        out_specs=vmem,
        scratch_shapes=[
            pltpu.VMEM((128, 2048), jnp.bfloat16),
            pltpu.VMEM((128, 2048), jnp.bfloat16),
            pltpu.VMEM((32, 32, 128), jnp.float32),
            pltpu.VMEM((16, 32, 128), jnp.float32),
            pltpu.VMEM((15, 32, 128), jnp.float32),
            pltpu.VMEM((8, 8, 128), jnp.float32),
            pltpu.VMEM((15, 8, 128), jnp.float32),
            pltpu.VMEM((32, 32, 256), jnp.bfloat16),
            dma, dma, dma((15,)), dma((15,)), dma((15,)), dma((15,)), dma((15,)), dma((15,)),
            dma((16,)), dma((16,)),
        ],
        compiler_params=pltpu.CompilerParams(
            collective_id=0, has_side_effects=True, vmem_limit_bytes=32 * 1024 * 1024),
    )(features, signs.reshape(1, -1), columns.reshape(8, 128), labels.reshape(1, 128))


def solution(mesh):
    in_specs = (P("tok", "feat"), P("feat"), P(), P("tok", None))
    out_specs = P("tok", "feat", None)
    return jax.shard_map(body, mesh=mesh, in_specs=in_specs, out_specs=out_specs, check_vma=False)
```

time: 1410 us -> 43.8 us (0.03)
  waiting for transfers between devices: 1330 us -> 0 us
  Pallas kernels: 0 us -> 40.4 us
  starting transfers between devices: 26.6 us -> 0 us
  matrix products: 25.3 us -> 0 us
    psum x1 -> x0, waiting for transfers between devices: 1110 us -> none  [body(): combined = lax.psum(jnp.where(owned, picked, 0.0), 'feat')]
    ppermute x6 -> x0, waiting for transfers between devices: 155 us -> none  [from_partner(): lax.ppermute(array, axis, [(i, i ^ 1 << distance) for i in range(lax.axis...]
    reduce_scatter x1 -> x0, waiting for transfers between devices: 68.5 us -> none  [body(): lax.psum_scatter(partial_gram.reshape(C // tok_count * lax.axis_size('tok...]
    pallas_call x0 -> x1, Pallas kernels: none -> 40.4 us  [body(): pl.pallas_call(kernel, out_shape=jax.ShapeDtypeStruct((4, 16, 1024), jnp....]
    ppermute x6 -> x0, starting transfers between devices: 26.5 us -> none  [from_partner(): lax.ppermute(array, axis, [(i, i ^ 1 << distance) for i in range(lax.axis...]
    dot_general x2 -> x0, matrix products: 25.3 us -> none  [the longest x1 23.5 us: body(): jnp.dot(signed, sylvester(width, jnp.bfloat16), preferred_element_type=jn...]
  transfers between devices with their start and end apart: 8 -> 0, of which waited for: 8 -> 0; matrix products, arithmetic and copies ran while one was open for 0% -> 0% of each run, Pallas kernels for 0% -> 0%
where the time goes in v1:
time: 43.8 us; the launch traced here: 43.6 us
  Pallas kernels  40.4 us (92%)
  local copies, waits for them, and re-layouts  3.13 us (7%)
    pallas_call x1, Pallas kernels, body(): pl.pallas_call(kernel, out_shape=jax.ShapeDtypeStruct((4, 16, 1024), jnp....  40.4 us
    unnamed x9, local copies, waits for them, and re-layouts  3.13 us

profile of v1, /device:TPU:1, one launch (start us, length us, event | category | flops | bytes accessed | tf_op | source)
XLA Modules:
  0.0 43.6 jit_solution(14695645801403817565)
XLA Ops:
  0.0 0.0 copy-start.2
  0.0 0.0 copy-start.3
  0.0 0.7 %copy-done.2 = s32[1024]{0:T(1024)S(1)} copy-done((s32[1024]{0:T(1024)S(1)}, s32[1024]{0:T(1024)}, u32[]{:S(2)}) %copy-start.2) | copy-done | bytes 4120
  0.7 0.0 copy-done.3
  0.7 0.0 copy-start
  0.7 1.0 %copy-done = bf16[128,2048]{1,0:T(8,128)(2,1)S(1)} copy-done((bf16[128,2048]{1,0:T(8,128)(2,1)S(1)}, bf16[128,2048]{1,0:T(8,128)(2,1)}, u32[]{:S(2)}) %copy-start) | copy-done | bytes 524312
  1.7 0.0 copy-start.1
  1.7 0.7 %copy-done.1 = s32[2048]{0:T(1024)S(1)} copy-done((s32[2048]{0:T(1024)S(1)}, s32[2048]{0:T(1024)}, u32[]{:S(2)}) %copy-start.1) | copy-done | bytes 8216
  2.4 40.4 %shard_map.46 = f32[4,16,1024]{2,1,0:T(8,128)S(1)} custom-call(bf16[128,2048]{1,0:T(8,128)(2,1)S(1)} %copy-done, s32[1,2048]{1,0:T(1,128)S(1)} %bitcast.3, s32[8,128]{1,0:T(8,128)S(1)} %bitcast.4, s32[1,128]{1,0:T(1,128)S(1)} %bitcast.5), custom_call_target="tpu_custom_call" | custom-call | tf_op jit(solution)/shard_map/pallas_call | solution.py:189
  42.9 0.7 %copy.6 = f32[4,16,1024]{2,1,0:T(8,128)} copy(f32[4,16,1024]{2,1,0:T(8,128)S(1)} %shard_map.46) | data formatting | bytes 524288
Async XLA Ops:
  0.0 0.7 %copy-start.2 = (s32[1024]{0:T(1024)S(1)}, s32[1024]{0:T(1024)}, u32[]{:S(2)}) copy-start(s32[1024]{0:T(1024)} %param.6) | copy-start | bytes 12292
  0.0 0.7 %copy-start.3 = (s32[128,1]{0,1:T(1,128)S(1)}, s32[128,1]{0,1:T(1,128)}, u32[]{:S(2)}) copy-start(s32[128,1]{0,1:T(1,128)} %param.7) | copy-start | bytes 1540
  0.7 1.0 %copy-start = (bf16[128,2048]{1,0:T(8,128)(2,1)S(1)}, bf16[128,2048]{1,0:T(8,128)(2,1)}, u32[]{:S(2)}) copy-start(bf16[128,2048]{1,0:T(8,128)(2,1)} %x_ref.1) | copy-start | bytes 1572868
  1.7 0.7 %copy-start.1 = (s32[2048]{0:T(1024)S(1)}, s32[2048]{0:T(1024)}, u32[]{:S(2)}) copy-start(s32[2048]{0:T(1024)} %param.5) | copy-start | bytes 24580

commit v2 on v1

--- a/solution.py
+++ b/solution.py
@@ -14,8 +14,16 @@
 NZ = NH * NG
 
 
-def kernel(x_ref, sg_ref, col_ref, lab_ref, out_ref, xs, s, y, r1, r2, fold, r3, g,
-           send1, recv1, send2, recv2, send3, recv3, send4, recv4, send5, recv5):
+FAR_XY = (10, 6, 14, 9, 11, 2, 8, 5, 7, 13, 15, 1, 3, 4, 12)
+FAR_Z = (8, 7, 9, 6, 10, 5, 11, 4, 12, 3, 13, 2, 14, 1, 15)
+
+
+def kernel(x_hbm, sg_hbm, col_hbm, lab_hbm, out_ref, x_ref, sg_ref, col_ref, lab_ref, xs, s, y, r1, r2, fold, r3, g,
+           rows32, give, take, load, send1, recv1, send2, recv2, send3, recv3, send4, recv4, send5, recv5, send6, recv6):
+    loads = [pltpu.make_async_copy(*pair, load.at[i]) for i, pair in enumerate(
+        ((x_hbm, x_ref), (sg_hbm, sg_ref), (col_hbm, col_ref), (lab_hbm, lab_ref)))]
+    for copy in loads:
+        copy.start()
     f = lax.axis_index("feat")
     tok = lax.axis_index("tok")
     core = f % NC
@@ -42,11 +50,13 @@
         return {"feat": feat_of(px, other // NG, py, core), "tok": other % NG}
 
     barrier = pltpu.get_barrier_semaphore()
+    for d in FAR_Z:
+        pl.semaphore_signal(barrier, inc=1, device_id=z_device(d), device_id_type=MESH)
+    for d in FAR_XY:
+        pl.semaphore_signal(barrier, inc=1, device_id=xy_device(d), device_id_type=MESH)
     pl.semaphore_signal(barrier, inc=1, device_id=sibling, device_id_type=MESH)
-    for d in range(1, NXY):
-        pl.semaphore_signal(barrier, inc=1, device_id=xy_device(d), device_id_type=MESH)
-    for d in range(1, NZ):
-        pl.semaphore_signal(barrier, inc=1, device_id=z_device(d), device_id_type=MESH)
+    for copy in loads:
+        copy.wait()
 
     xs[...] = x_ref[...] * sg_ref[...].astype(jnp.float32).astype(jnp.bfloat16)
     lane = lax.broadcasted_iota(jnp.int32, (128, 128), 1)
@@ -92,7 +102,7 @@
 
     pair.wait_recv()
     out2 = []
-    for d in range(1, NXY):
+    for d in FAR_XY:
         qx, qy = xy_at(d)
         there = qx * NY + qy
         mine = NXY * core + there
@@ -103,8 +113,9 @@
         copy.start()
         out2.append(copy)
     total = y[NXY * core + xy] + r1[xy]
+    for copy, d in zip(out2, FAR_XY):
+        copy.wait_recv()
     for d in range(1, NXY):
-        out2[d - 1].wait_recv()
         total = total + r2[d - 1]
 
     hi = total.astype(jnp.bfloat16)
@@ -120,14 +131,14 @@
             tile = jnp.where(quarter == k, picked[8 * k:8 * k + 8, 128 * q:128 * q + 128], tile)
         fold[q] = tile
     out3 = []
-    for d in range(1, NZ):
+    for d in FAR_Z:
         copy = pltpu.make_async_remote_copy(
             src_ref=fold.at[(plane + d) % NG], dst_ref=r3.at[d - 1], send_sem=send3.at[d - 1],
             recv_sem=recv3.at[d - 1], device_id=z_device(d), device_id_type=MESH)
         copy.start()
         out3.append(copy)
-    for d in range(1, NZ):
-        out3[d - 1].wait_recv()
+    for copy in out3:
+        copy.wait_recv()
     scale = 1.0 / math.sqrt(131072)
     tiles = []
     for d in range(NG):
@@ -145,42 +156,66 @@
                 piece = moved if piece is None else jnp.where(quarter == j, moved, piece)
             halves.append(piece)
         rows.append(jnp.concatenate(halves, axis=1))
-    mine = NXY * core + xy
-    g[mine] = jnp.concatenate(rows, axis=0).astype(jnp.bfloat16)
-
-    out5 = []
-
-    def forward(d, block):
-        copy = pltpu.make_async_remote_copy(
-            src_ref=g.at[block], dst_ref=g.at[block], send_sem=send5.at[d], recv_sem=recv5.at[d],
-            device_id=sibling, device_id_type=MESH)
-        copy.start()
-        out5.append(copy)
-
-    out4 = []
-    for d in range(1, NXY):
-        copy = pltpu.make_async_remote_copy(
-            src_ref=g.at[mine], dst_ref=g.at[mine], send_sem=send4.at[d - 1], recv_sem=recv4.at[d - 1],
+    g[xy] = jnp.concatenate(rows, axis=0).astype(jnp.bfloat16)
+
+    out4 = {}
+    for d in FAR_XY:
+        out4[d] = pltpu.make_async_remote_copy(
+            src_ref=g.at[xy], dst_ref=g.at[xy], send_sem=send4.at[d - 1], recv_sem=recv4.at[d - 1],
             device_id=xy_device(d), device_id_type=MESH)
-        copy.start()
-        out4.append(copy)
-    forward(0, mine)
-    for d in range(1, NXY):
-        out4[d - 1].wait_recv()
-        came = (px - d // NY + NX) % NX * NY + (py - d % NY + NY) % NY
-        forward(d, NXY * core + came)
-    for copy in out5:
-        copy.wait_recv()
-
-    own = g[f // 2, pl.ds(pl.multiple_of(f % 2 * 16, 16), 16), :]
+        out4[d].start()
+
+    wanted = 8 * px + 4 * zh + py
+    holder = wanted // NXY == core
+    where = wanted % NXY
+    hand = pltpu.make_async_remote_copy(
+        src_ref=g.at[where], dst_ref=rows32, send_sem=send5, recv_sem=recv5,
+        device_id=sibling, device_id_type=MESH)
+    shift = (px - where // NY + NX) % NX
+
+    @pl.when(holder & (shift == 0))
+    def _():
+        hand.start()
+
+    for step in (1, 3, 2):
+        out4[NY * step].wait_recv()
+
+        @pl.when(holder & (shift == step))
+        def _():
+            hand.start()
+
+    for d in FAR_XY[::-1]:
+        if d % NY:
+            out4[d].wait_recv()
+
+    @pl.when(holder)
+    def _():
+        hand.wait_send()
+        rows32[...] = g[where]
+
+    @pl.when(jnp.logical_not(holder))
+    def _():
+        hand.wait_recv()
+
     concept = lax.broadcasted_iota(jnp.int32, (16, 256), 1) % 32 // 8
-    left = jnp.concatenate([jnp.where(concept == k, own, jnp.zeros_like(own)) for k in range(4)], axis=0)
-    gram = lax.dot_general(left, g[...].reshape(1024, 256), (((1,), (1,)), ((), ())),
-                           preferred_element_type=jnp.float32)
-    out_ref[...] = (gram * (C / 1024)).reshape(4, 16, 1024)
-    pair.wait_send()
-    for copy in out2 + out3 + out4 + out5:
+    half = g[...].reshape(512, 256)
+
+    def gram(part):
+        own = rows32[pl.ds(pl.multiple_of(16 * part, 16), 16), :]
+        left = jnp.concatenate([jnp.where(concept == k, own, jnp.zeros_like(own)) for k in range(4)], axis=0)
+        found = lax.dot_general(left, half, (((1,), (1,)), ((), ())), preferred_element_type=jnp.float32)
+        return found * (C / 1024)
+
+    give[...] = gram(1 - core)
+    swap = pltpu.make_async_remote_copy(
+        src_ref=give, dst_ref=take, send_sem=send6, recv_sem=recv6, device_id=sibling, device_id_type=MESH)
+    swap.start()
+    out_ref[:, :, pl.ds(pl.multiple_of(512 * core, 512), 512)] = gram(core).reshape(4, 16, 512)
+    for copy in [pair] + out2 + out3 + list(out4.values()):
         copy.wait_send()
+    swap.wait_recv()
+    out_ref[:, :, pl.ds(pl.multiple_of(512 * (1 - core), 512), 512)] = take[...].reshape(4, 16, 512)
+    swap.wait_send()
 
 
 def body(features, signs, columns, labels):
@@ -189,9 +224,13 @@
     return pl.pallas_call(
         kernel,
         out_shape=jax.ShapeDtypeStruct((4, 16, 1024), jnp.float32),
-        in_specs=[vmem] * 4,
+        in_specs=[pl.BlockSpec(memory_space=pltpu.HBM)] * 4,
         out_specs=vmem,
         scratch_shapes=[
+            pltpu.VMEM((128, 2048), jnp.bfloat16),
+            pltpu.VMEM((1, 2048), jnp.int32),
+            pltpu.VMEM((8, 128), jnp.int32),
+            pltpu.VMEM((1, 128), jnp.int32),
             pltpu.VMEM((128, 2048), jnp.bfloat16),
             pltpu.VMEM((128, 2048), jnp.bfloat16),
             pltpu.VMEM((32, 32, 128), jnp.float32),
@@ -199,12 +238,15 @@
             pltpu.VMEM((15, 32, 128), jnp.float32),
             pltpu.VMEM((8, 8, 128), jnp.float32),
             pltpu.VMEM((15, 8, 128), jnp.float32),
-            pltpu.VMEM((32, 32, 256), jnp.bfloat16),
-            dma, dma, dma((15,)), dma((15,)), dma((15,)), dma((15,)), dma((15,)), dma((15,)),
-            dma((16,)), dma((16,)),
+            pltpu.VMEM((16, 32, 256), jnp.bfloat16),
+            pltpu.VMEM((32, 256), jnp.bfloat16),
+            pltpu.VMEM((64, 512), jnp.float32),
+            pltpu.VMEM((64, 512), jnp.float32),
+            dma((4,)), dma, dma, dma((15,)), dma((15,)), dma((15,)), dma((15,)), dma((15,)), dma((15,)),
+            dma, dma, dma, dma,
         ],
         compiler_params=pltpu.CompilerParams(
-            collective_id=0, has_side_effects=True, vmem_limit_bytes=32 * 1024 * 1024),
+            collective_id=0, has_side_effects=True, vmem_limit_bytes=54784 * 1024),
     )(features, signs.reshape(1, -1), columns.reshape(8, 128), labels.reshape(1, 128))
 
 

time: 43.8 us -> 41.1 us (0.938)
  Pallas kernels: 40.4 us -> 38.8 us
  local copies, waits for them, and re-layouts: 3.13 us -> 2.09 us
    pallas_call x1, Pallas kernels: 40.4 us -> 38.8 us  [body(): pl.pallas_call(kernel, out_shape=jax.ShapeDtypeStruct((4, 16, 1024), jnp....]
    unnamed x9 -> x7, local copies, waits for them, and re-layouts: 3.13 us -> 2.09 us
where the time goes in v2:
time: 41.1 us; the launch traced here: 40.9 us
  Pallas kernels  38.8 us (94%)
  local copies, waits for them, and re-layouts  2.09 us (5%)
    pallas_call x1, Pallas kernels, body(): pl.pallas_call(kernel, out_shape=jax.ShapeDtypeStruct((4, 16, 1024), jnp....  38.8 us
    unnamed x7, local copies, waits for them, and re-layouts  2.09 us

profile of v2, /device:TPU:1, one launch (start us, length us, event | category | flops | bytes accessed | tf_op | source)
XLA Modules:
  0.0 40.9 jit_solution(13900118802382020884)
XLA Ops:
  0.0 0.0 copy-start.1
  0.0 0.0 copy-start.2
  0.0 0.7 %copy-done.1 = s32[1024]{0:T(1024)S(1)} copy-done((s32[1024]{0:T(1024)S(1)}, s32[1024]{0:T(1024)}, u32[]{:S(2)}) %copy-start.1) | copy-done | bytes 4120
  0.7 0.0 copy-done.2
  0.7 0.0 copy-start
  0.7 0.7 %copy-done = s32[2048]{0:T(1024)S(1)} copy-done((s32[2048]{0:T(1024)S(1)}, s32[2048]{0:T(1024)}, u32[]{:S(2)}) %copy-start) | copy-done | bytes 8216
  1.4 38.8 %shard_map.46 = f32[4,16,1024]{2,1,0:T(8,128)S(1)} custom-call(bf16[128,2048]{1,0:T(8,128)(2,1)} %x_hbm.1, s32[1,2048]{1,0:T(1,128)S(1)} %bitcast.3, s32[8,128]{1,0:T(8,128)S(1)} %bitcast.4, s32[1,128]{1,0:T(1,128)S(1)} %bitcast.5), custom_call_target="tpu_custom_call" | custom-call | tf_op jit(solution)/shard_map/pallas_call | solution.py:224
  40.2 0.7 %copy.6 = f32[4,16,1024]{2,1,0:T(8,128)} copy(f32[4,16,1024]{2,1,0:T(8,128)S(1)} %shard_map.46) | data formatting | bytes 524288
Async XLA Ops:
  0.0 0.7 %copy-start.1 = (s32[1024]{0:T(1024)S(1)}, s32[1024]{0:T(1024)}, u32[]{:S(2)}) copy-start(s32[1024]{0:T(1024)} %param.6) | copy-start | bytes 12292
  0.0 0.7 %copy-start.2 = (s32[128,1]{0,1:T(1,128)S(1)}, s32[128,1]{0,1:T(1,128)}, u32[]{:S(2)}) copy-start(s32[128,1]{0,1:T(1,128)} %param.7) | copy-start | bytes 1540
  0.7 0.7 %copy-start = (s32[2048]{0:T(1024)S(1)}, s32[2048]{0:T(1024)}, u32[]{:S(2)}) copy-start(s32[2048]{0:T(1024)} %param.5) | copy-start | bytes 24580

commit v3 on v2

--- a/solution.py
+++ b/solution.py
@@ -18,8 +18,9 @@
 FAR_Z = (8, 7, 9, 6, 10, 5, 11, 4, 12, 3, 13, 2, 14, 1, 15)
 
 
-def kernel(x_hbm, sg_hbm, col_hbm, lab_hbm, out_ref, x_ref, sg_ref, col_ref, lab_ref, xs, s, y, r1, r2, fold, r3, g,
-           rows32, give, take, load, send1, recv1, send2, recv2, send3, recv3, send4, recv4, send5, recv5, send6, recv6):
+def kernel(x_hbm, sg_hbm, col_hbm, lab_hbm, out_ref, x_ref, sg_ref, col_ref, lab_ref, xs, s, flip, y, r1, r2, fold, r3, g,
+           rows32, give, take, load, send1, recv1, send2, recv2, send3, recv3, send4, recv4, send5, recv5, send6, recv6,
+           plane_here, line_here):
     loads = [pltpu.make_async_copy(*pair, load.at[i]) for i, pair in enumerate(
         ((x_hbm, x_ref), (sg_hbm, sg_ref), (col_hbm, col_ref), (lab_hbm, lab_ref)))]
     for copy in loads:
@@ -41,54 +42,74 @@
     def xy_at(d):
         return (px + d // NY) % NX, (py + d % NY) % NY
 
-    def xy_device(d):
+    def xy_device(d, c):
         qx, qy = xy_at(d)
-        return {"feat": feat_of(qx, zh, qy, core), "tok": tok}
-
-    def z_device(d):
+        return {"feat": feat_of(qx, zh, qy, c), "tok": tok}
+
+    def z_device(d, c):
         other = (plane + d) % NZ
-        return {"feat": feat_of(px, other // NG, py, core), "tok": other % NG}
+        return {"feat": feat_of(px, other // NG, py, c), "tok": other % NG}
+
+    def signal(sem, device):
+        pl.semaphore_signal(sem, inc=1, device_id=device, device_id_type=MESH)
 
     barrier = pltpu.get_barrier_semaphore()
+    for d in FAR_XY:
+        signal(barrier, xy_device(d, 0))
+
+    @pl.when(core == 1)
+    def _():
+        signal(barrier, sibling)
+
     for d in FAR_Z:
-        pl.semaphore_signal(barrier, inc=1, device_id=z_device(d), device_id_type=MESH)
-    for d in FAR_XY:
-        pl.semaphore_signal(barrier, inc=1, device_id=xy_device(d), device_id_type=MESH)
-    pl.semaphore_signal(barrier, inc=1, device_id=sibling, device_id_type=MESH)
-    for copy in loads:
-        copy.wait()
-
-    xs[...] = x_ref[...] * sg_ref[...].astype(jnp.float32).astype(jnp.bfloat16)
+        signal(barrier, z_device(d, 1))
+
+    loads[2].wait()
     lane = lax.broadcasted_iota(jnp.int32, (128, 128), 1)
 
-    def chunk(i):
+    @pl.loop(0, 8)
+    def _(i):
         c = jnp.broadcast_to(col_ref[pl.ds(i, 1), :], (128, 128)).T
         v = (c & lane) ^ (c >> 11 & f)
         v = v ^ v >> 4
         v = v ^ v >> 2
         v = v ^ v >> 1
         parts = [(1 - 2 * (v & 1)).astype(jnp.float32).astype(jnp.bfloat16)]
-        for bit in range(4):
-            flip = (1 - 2 * (c >> 7 + bit & 1)).astype(jnp.float32).astype(jnp.bfloat16)
-            parts = parts + [part * flip for part in parts]
-        for block in range(16):
-            s[:, 128 * block:128 * block + 128] = parts[block]
-        found = lax.dot_general(s[...], xs[...], (((1,), (1,)), ((), ())), preferred_element_type=jnp.float32)
-        y[pl.ds(4 * i, 4)] = found.reshape(4, 32, 128)
-
-    @pl.loop(0, 4)
-    def _(n):
-        chunk(4 * (1 - core) + n)
-
-    pl.semaphore_wait(barrier, 1 + (NXY - 1) + (NZ - 1))
+        for bit in range(3):
+            turn = (1 - 2 * (c >> 7 + bit & 1)).astype(jnp.float32).astype(jnp.bfloat16)
+            parts = parts + [part * turn for part in parts]
+        for block in range(8):
+            s[i, :, 128 * block:128 * block + 128] = parts[block]
+        flip[i] = (1 - 2 * (c >> 10 & 1)).astype(jnp.float32)
+
+    for i in (0, 1, 3):
+        loads[i].wait()
+    sign = sg_ref[...].astype(jnp.float32).astype(jnp.bfloat16)
+    for h in range(2):
+        xs[128 * h:128 * h + 128, :] = x_ref[:, 1024 * h:1024 * h + 1024] * sign[:, 1024 * h:1024 * h + 1024]
+
+    def half_of(c):
+        kept = s[pl.ds(4 * c, 4)].reshape(512, 1024)
+        found = lax.dot_general(kept, xs[...], (((1,), (1,)), ((), ())), preferred_element_type=jnp.float32)
+        found = found[:, :128] + found[:, 128:] * flip[pl.ds(4 * c, 4)].reshape(512, 128)
+        y[pl.ds(NXY * c, NXY)] = found.reshape(NXY, 32, 128)
+
+    half_of(1 - core)
+
+    @pl.when(core == 0)
+    def _():
+        pl.semaphore_wait(barrier, 2 * (NXY - 1) + 1)
+        signal(plane_here, sibling)
+
+    @pl.when(core == 1)
+    def _():
+        pl.semaphore_wait(plane_here, 1)
+
     pair = pltpu.make_async_remote_copy(
         src_ref=y.at[pl.ds(NXY * (1 - core), NXY)], dst_ref=r1, send_sem=send1, recv_sem=recv1,
         device_id=sibling, device_id_type=MESH)
     pair.start()
-
-    @pl.loop(0, 4)
-    def _(n):
-        chunk(4 * core + n)
+    half_of(core)
 
     row = jnp.broadcast_to(lab_ref[...], (128, 128))
     col = row.T
@@ -109,10 +130,20 @@
         y[mine] = y[mine] + r1[there]
         copy = pltpu.make_async_remote_copy(
             src_ref=y.at[mine], dst_ref=r2.at[d - 1], send_sem=send2.at[d - 1], recv_sem=recv2.at[d - 1],
-            device_id=xy_device(d), device_id_type=MESH)
+            device_id=xy_device(d, core), device_id_type=MESH)
         copy.start()
         out2.append(copy)
     total = y[NXY * core + xy] + r1[xy]
+
+    @pl.when(core == 1)
+    def _():
+        pl.semaphore_wait(barrier, 2 * (NZ - 1))
+        signal(line_here, sibling)
+
+    @pl.when(core == 0)
+    def _():
+        pl.semaphore_wait(line_here, 1)
+
     for copy, d in zip(out2, FAR_XY):
         copy.wait_recv()
     for d in range(1, NXY):
@@ -134,7 +165,7 @@
     for d in FAR_Z:
         copy = pltpu.make_async_remote_copy(
             src_ref=fold.at[(plane + d) % NG], dst_ref=r3.at[d - 1], send_sem=send3.at[d - 1],
-            recv_sem=recv3.at[d - 1], device_id=z_device(d), device_id_type=MESH)
+            recv_sem=recv3.at[d - 1], device_id=z_device(d, core), device_id_type=MESH)
         copy.start()
         out3.append(copy)
     for copy in out3:
@@ -162,7 +193,7 @@
     for d in FAR_XY:
         out4[d] = pltpu.make_async_remote_copy(
             src_ref=g.at[xy], dst_ref=g.at[xy], send_sem=send4.at[d - 1], recv_sem=recv4.at[d - 1],
-            device_id=xy_device(d), device_id_type=MESH)
+            device_id=xy_device(d, core), device_id_type=MESH)
         out4[d].start()
 
     wanted = 8 * px + 4 * zh + py
@@ -184,10 +215,6 @@
         def _():
             hand.start()
 
-    for d in FAR_XY[::-1]:
-        if d % NY:
-            out4[d].wait_recv()
-
     @pl.when(holder)
     def _():
         hand.wait_send()
@@ -198,24 +225,36 @@
         hand.wait_recv()
 
     concept = lax.broadcasted_iota(jnp.int32, (16, 256), 1) % 32 // 8
-    half = g[...].reshape(512, 256)
-
-    def gram(part):
+
+    def left_of(part):
         own = rows32[pl.ds(pl.multiple_of(16 * part, 16), 16), :]
-        left = jnp.concatenate([jnp.where(concept == k, own, jnp.zeros_like(own)) for k in range(4)], axis=0)
-        found = lax.dot_general(left, half, (((1,), (1,)), ((), ())), preferred_element_type=jnp.float32)
-        return found * (C / 1024)
-
-    give[...] = gram(1 - core)
-    swap = pltpu.make_async_remote_copy(
-        src_ref=give, dst_ref=take, send_sem=send6, recv_sem=recv6, device_id=sibling, device_id_type=MESH)
-    swap.start()
-    out_ref[:, :, pl.ds(pl.multiple_of(512 * core, 512), 512)] = gram(core).reshape(4, 16, 512)
+        return [jnp.where(concept == k, own, jnp.zeros_like(own)) for k in range(4)]
+
+    left = jnp.concatenate(left_of(1 - core) + left_of(core), axis=0)
+    swaps = []
+    for step in (0, 1, 3, 2):
+        for dy in (1, 3, 2):
+            out4[NY * step + dy].wait_recv()
+        came = (px - step + NX) % NX
+        quarter_rows = g[pl.ds(4 * came, 4)].reshape(128, 256)
+        found = lax.dot_general(left, quarter_rows, (((1,), (1,)), ((), ())), preferred_element_type=jnp.float32)
+        found = found * (C / 1024)
+        give[step] = found[:64]
+        swap = pltpu.make_async_remote_copy(
+            src_ref=give.at[step], dst_ref=take.at[step], send_sem=send6.at[step], recv_sem=recv6.at[step],
+            device_id=sibling, device_id_type=MESH)
+        swap.start()
+        swaps.append((swap, step, came))
+        at = pl.multiple_of(512 * core + 128 * came, 128)
+        out_ref[:, :, pl.ds(at, 128)] = found[64:].reshape(4, 16, 128)
     for copy in [pair] + out2 + out3 + list(out4.values()):
         copy.wait_send()
-    swap.wait_recv()
-    out_ref[:, :, pl.ds(pl.multiple_of(512 * (1 - core), 512), 512)] = take[...].reshape(4, 16, 512)
-    swap.wait_send()
+    for swap, step, came in swaps:
+        swap.wait_recv()
+        at = pl.multiple_of(512 * (1 - core) + 128 * came, 128)
+        out_ref[:, :, pl.ds(at, 128)] = take[step].reshape(4, 16, 128)
+    for swap, step, came in swaps:
+        swap.wait_send()
 
 
 def body(features, signs, columns, labels):
@@ -231,8 +270,9 @@
             pltpu.VMEM((1, 2048), jnp.int32),
             pltpu.VMEM((8, 128), jnp.int32),
             pltpu.VMEM((1, 128), jnp.int32),
-            pltpu.VMEM((128, 2048), jnp.bfloat16),
-            pltpu.VMEM((128, 2048), jnp.bfloat16),
+            pltpu.VMEM((256, 1024), jnp.bfloat16),
+            pltpu.VMEM((8, 128, 1024), jnp.bfloat16),
+            pltpu.VMEM((8, 128, 128), jnp.float32),
             pltpu.VMEM((32, 32, 128), jnp.float32),
             pltpu.VMEM((16, 32, 128), jnp.float32),
             pltpu.VMEM((15, 32, 128), jnp.float32),
@@ -240,10 +280,10 @@
             pltpu.VMEM((15, 8, 128), jnp.float32),
             pltpu.VMEM((16, 32, 256), jnp.bfloat16),
             pltpu.VMEM((32, 256), jnp.bfloat16),
-            pltpu.VMEM((64, 512), jnp.float32),
-            pltpu.VMEM((64, 512), jnp.float32),
+            pltpu.VMEM((4, 64, 128), jnp.float32),
+            pltpu.VMEM((4, 64, 128), jnp.float32),
             dma((4,)), dma, dma, dma((15,)), dma((15,)), dma((15,)), dma((15,)), dma((15,)), dma((15,)),
-            dma, dma, dma, dma,
+            dma, dma, dma((4,)), dma((4,)), pltpu.SemaphoreType.REGULAR, pltpu.SemaphoreType.REGULAR,
         ],
         compiler_params=pltpu.CompilerParams(
             collective_id=0, has_side_effects=True, vmem_limit_bytes=54784 * 1024),

time: 41.1 us -> 41 us (level)
  no operation moved by 1% of the time
where the time goes in v3:
time: 41 us; the launch traced here: 40.8 us
  Pallas kernels  38.7 us (94%)
  local copies, waits for them, and re-layouts  2.09 us (5%)
    pallas_call x1, Pallas kernels, body(): pl.pallas_call(kernel, out_shape=jax.ShapeDtypeStruct((4, 16, 1024), jnp....  38.7 us
    unnamed x7, local copies, waits for them, and re-layouts  2.09 us

profile of v3, /device:TPU:1, one launch (start us, length us, event | category | flops | bytes accessed | tf_op | source)
XLA Modules:
  0.0 40.8 jit_solution(11623251822125343781)
XLA Ops:
  0.0 0.0 copy-start.1
  0.0 0.0 copy-start.2
  0.0 0.7 %copy-done.1 = s32[1024]{0:T(1024)S(1)} copy-done((s32[1024]{0:T(1024)S(1)}, s32[1024]{0:T(1024)}, u32[]{:S(2)}) %copy-start.1) | copy-done | bytes 4120
  0.7 0.0 copy-done.2
  0.7 0.0 copy-start
  0.7 0.7 %copy-done = s32[2048]{0:T(1024)S(1)} copy-done((s32[2048]{0:T(1024)S(1)}, s32[2048]{0:T(1024)}, u32[]{:S(2)}) %copy-start) | copy-done | bytes 8216
  1.4 38.7 %shard_map.46 = f32[4,16,1024]{2,1,0:T(8,128)S(1)} custom-call(bf16[128,2048]{1,0:T(8,128)(2,1)} %x_hbm.1, s32[1,2048]{1,0:T(1,128)S(1)} %bitcast.3, s32[8,128]{1,0:T(8,128)S(1)} %bitcast.4, s32[1,128]{1,0:T(1,128)S(1)} %bitcast.5), custom_call_target="tpu_custom_call" | custom-call | tf_op jit(solution)/shard_map/pallas_call | solution.py:263
  40.1 0.7 %copy.6 = f32[4,16,1024]{2,1,0:T(8,128)} copy(f32[4,16,1024]{2,1,0:T(8,128)S(1)} %shard_map.46) | data formatting | bytes 524288
Async XLA Ops:
  0.0 0.7 %copy-start.1 = (s32[1024]{0:T(1024)S(1)}, s32[1024]{0:T(1024)}, u32[]{:S(2)}) copy-start(s32[1024]{0:T(1024)} %param.6) | copy-start | bytes 12292
  0.0 0.7 %copy-start.2 = (s32[128,1]{0,1:T(1,128)S(1)}, s32[128,1]{0,1:T(1,128)}, u32[]{:S(2)}) copy-start(s32[128,1]{0,1:T(1,128)} %param.7) | copy-start | bytes 1540
  0.7 0.7 %copy-start = (s32[2048]{0:T(1024)S(1)}, s32[2048]{0:T(1024)}, u32[]{:S(2)}) copy-start(s32[2048]{0:T(1024)} %param.5) | copy-start | bytes 24580

commit v4 on v3

--- a/solution.py
+++ b/solution.py
@@ -22,7 +22,8 @@
            rows32, give, take, load, send1, recv1, send2, recv2, send3, recv3, send4, recv4, send5, recv5, send6, recv6,
            plane_here, line_here):
     loads = [pltpu.make_async_copy(*pair, load.at[i]) for i, pair in enumerate(
-        ((x_hbm, x_ref), (sg_hbm, sg_ref), (col_hbm, col_ref), (lab_hbm, lab_ref)))]
+        [(col_hbm, col_ref), (sg_hbm, sg_ref), (lab_hbm, lab_ref)]
+        + [(x_hbm.at[pl.ds(16 * k, 16)], x_ref.at[pl.ds(16 * k, 16)]) for k in range(8)])]
     for copy in loads:
         copy.start()
     f = lax.axis_index("feat")
@@ -64,7 +65,7 @@
     for d in FAR_Z:
         signal(barrier, z_device(d, 1))
 
-    loads[2].wait()
+    loads[0].wait()
     lane = lax.broadcasted_iota(jnp.int32, (128, 128), 1)
 
     @pl.loop(0, 8)
@@ -82,8 +83,8 @@
             s[i, :, 128 * block:128 * block + 128] = parts[block]
         flip[i] = (1 - 2 * (c >> 10 & 1)).astype(jnp.float32)
 
-    for i in (0, 1, 3):
-        loads[i].wait()
+    for copy in loads[1:]:
+        copy.wait()
     sign = sg_ref[...].astype(jnp.float32).astype(jnp.bfloat16)
     for h in range(2):
         xs[128 * h:128 * h + 128, :] = x_ref[:, 1024 * h:1024 * h + 1024] * sign[:, 1024 * h:1024 * h + 1024]
@@ -258,6 +259,7 @@
 
 
 def body(features, signs, columns, labels):
+    args = features, signs.reshape(1, -1), columns.reshape(8, 128), labels.reshape(1, 128)
     vmem = pl.BlockSpec(memory_space=pltpu.VMEM)
     dma = pltpu.SemaphoreType.DMA
     return pl.pallas_call(
@@ -282,12 +284,12 @@
             pltpu.VMEM((32, 256), jnp.bfloat16),
             pltpu.VMEM((4, 64, 128), jnp.float32),
             pltpu.VMEM((4, 64, 128), jnp.float32),
-            dma((4,)), dma, dma, dma((15,)), dma((15,)), dma((15,)), dma((15,)), dma((15,)), dma((15,)),
+            dma((11,)), dma, dma, dma((15,)), dma((15,)), dma((15,)), dma((15,)), dma((15,)), dma((15,)),
             dma, dma, dma((4,)), dma((4,)), pltpu.SemaphoreType.REGULAR, pltpu.SemaphoreType.REGULAR,
         ],
         compiler_params=pltpu.CompilerParams(
-            collective_id=0, has_side_effects=True, vmem_limit_bytes=54784 * 1024),
-    )(features, signs.reshape(1, -1), columns.reshape(8, 128), labels.reshape(1, 128))
+            collective_id=0, has_side_effects=True, vmem_limit_bytes=40 * 1024 * 1024),
+    )(*[pltpu.with_memory_space_constraint(arg, pltpu.HBM) for arg in args])
 
 
 def solution(mesh):

time: 41 us -> 39.6 us (0.966)
  local copies, waits for them, and re-layouts: 2.09 us -> 0.71 us
    unnamed x7 -> x1, local copies, waits for them, and re-layouts: 2.09 us -> 0.71 us
where the time goes in v4:
time: 39.6 us; the launch traced here: 39.5 us
  Pallas kernels  38.8 us (98%)
  local copies, waits for them, and re-layouts  0.71 us (2%)
    pallas_call x1, Pallas kernels, body(): pl.pallas_call(kernel, out_shape=jax.ShapeDtypeStruct((4, 16, 1024), jnp....  38.8 us

profile of v4, /device:TPU:1, one launch (start us, length us, event | category | flops | bytes accessed | tf_op | source)
XLA Modules:
  0.0 39.5 jit_solution(4197337301679485771)
XLA Ops:
  0.0 38.8 %shard_map.46 = f32[4,16,1024]{2,1,0:T(8,128)S(1)} custom-call(bf16[128,2048]{1,0:T(8,128)(2,1)} %x_hbm.1, s32[1,2048]{1,0:T(1,128)} %bitcast.3, s32[8,128]{1,0:T(8,128)} %bitcast.4, s32[1,128]{1,0:T(1,128)} %bitcast.5), custom_call_target="tpu_custom_call" | custom-call | tf_op jit(solution)/shard_map/pallas_call | solution.py:265
  38.8 0.7 %copy.6 = f32[4,16,1024]{2,1,0:T(8,128)} copy(f32[4,16,1024]{2,1,0:T(8,128)S(1)} %shard_map.46) | data formatting | bytes 524288

commit v5 on v4

--- a/solution.py
+++ b/solution.py
@@ -15,12 +15,13 @@
 
 
 FAR_XY = (10, 6, 14, 9, 11, 2, 8, 5, 7, 13, 15, 1, 3, 4, 12)
+STEPS = (2, 1, 3, 0)
 FAR_Z = (8, 7, 9, 6, 10, 5, 11, 4, 12, 3, 13, 2, 14, 1, 15)
 
 
 def kernel(x_hbm, sg_hbm, col_hbm, lab_hbm, out_ref, x_ref, sg_ref, col_ref, lab_ref, xs, s, flip, y, r1, r2, fold, r3, g,
            rows32, give, take, load, send1, recv1, send2, recv2, send3, recv3, send4, recv4, send5, recv5, send6, recv6,
-           plane_here, line_here):
+           both_here, all_here):
     loads = [pltpu.make_async_copy(*pair, load.at[i]) for i, pair in enumerate(
         [(col_hbm, col_ref), (sg_hbm, sg_ref), (lab_hbm, lab_ref)]
         + [(x_hbm.at[pl.ds(16 * k, 16)], x_ref.at[pl.ds(16 * k, 16)]) for k in range(8)])]
@@ -55,33 +56,40 @@
         pl.semaphore_signal(sem, inc=1, device_id=device, device_id_type=MESH)
 
     barrier = pltpu.get_barrier_semaphore()
+
+    @pl.when(core == 0)
+    def _():
+        signal(barrier, sibling)
+
+    for d in FAR_Z:
+        signal(barrier, z_device(d, 0))
     for d in FAR_XY:
         signal(barrier, xy_device(d, 0))
 
     @pl.when(core == 1)
     def _():
-        signal(barrier, sibling)
-
-    for d in FAR_Z:
-        signal(barrier, z_device(d, 1))
+        pl.semaphore_wait(barrier, 1)
+        signal(both_here, sibling)
 
     loads[0].wait()
     lane = lax.broadcasted_iota(jnp.int32, (128, 128), 1)
-
-    @pl.loop(0, 8)
-    def _(i):
-        c = jnp.broadcast_to(col_ref[pl.ds(i, 1), :], (128, 128)).T
-        v = (c & lane) ^ (c >> 11 & f)
-        v = v ^ v >> 4
-        v = v ^ v >> 2
-        v = v ^ v >> 1
+    kept_at = col_ref[...]
+    high = kept_at >> 11 & f
+    for shift in (4, 2, 1):
+        high = high ^ high >> shift
+    code = kept_at & 127 | (high & 1) << 7 | (kept_at & 1920) << 1
+    for i in range(8):
+        c = jnp.broadcast_to(code[i:i + 1, :], (128, 128)).T
+        v = c & (lane | 128)
+        for shift in (4, 2, 1):
+            v = v ^ v >> shift
         parts = [(1 - 2 * (v & 1)).astype(jnp.float32).astype(jnp.bfloat16)]
         for bit in range(3):
-            turn = (1 - 2 * (c >> 7 + bit & 1)).astype(jnp.float32).astype(jnp.bfloat16)
+            turn = (1 - 2 * (c >> 8 + bit & 1)).astype(jnp.float32).astype(jnp.bfloat16)
             parts = parts + [part * turn for part in parts]
         for block in range(8):
             s[i, :, 128 * block:128 * block + 128] = parts[block]
-        flip[i] = (1 - 2 * (c >> 10 & 1)).astype(jnp.float32)
+        flip[i] = (1 - 2 * (c >> 11 & 1)).astype(jnp.float32)
 
     for copy in loads[1:]:
         copy.wait()
@@ -99,17 +107,15 @@
 
     @pl.when(core == 0)
     def _():
-        pl.semaphore_wait(barrier, 2 * (NXY - 1) + 1)
-        signal(plane_here, sibling)
-
-    @pl.when(core == 1)
-    def _():
-        pl.semaphore_wait(plane_here, 1)
-
-    pair = pltpu.make_async_remote_copy(
-        src_ref=y.at[pl.ds(NXY * (1 - core), NXY)], dst_ref=r1, send_sem=send1, recv_sem=recv1,
-        device_id=sibling, device_id_type=MESH)
-    pair.start()
+        pl.semaphore_wait(both_here, 1)
+
+    pairs = []
+    for k, step in enumerate(STEPS):
+        there = 4 * ((px + step) % NX)
+        pairs.append(pltpu.make_async_remote_copy(
+            src_ref=y.at[pl.ds(NXY * (1 - core) + there, 4)], dst_ref=r1.at[pl.ds(there, 4)],
+            send_sem=send1.at[k], recv_sem=recv1.at[k], device_id=sibling, device_id_type=MESH))
+        pairs[k].start()
     half_of(core)
 
     row = jnp.broadcast_to(lab_ref[...], (128, 128))
@@ -122,30 +128,31 @@
     spread = jnp.concatenate(
         [jnp.where(slot == within + 32.0 * q, 1.0, 0.0).astype(jnp.bfloat16) for q in range(NG)], axis=1)
 
-    pair.wait_recv()
+    @pl.when(core == 0)
+    def _():
+        pl.semaphore_wait(barrier, 2 * (NXY - 1) + 2 * (NZ - 1))
+        signal(all_here, sibling)
+
+    @pl.when(core == 1)
+    def _():
+        pl.semaphore_wait(all_here, 1)
+
     out2 = []
-    for d in FAR_XY:
-        qx, qy = xy_at(d)
-        there = qx * NY + qy
-        mine = NXY * core + there
-        y[mine] = y[mine] + r1[there]
-        copy = pltpu.make_async_remote_copy(
-            src_ref=y.at[mine], dst_ref=r2.at[d - 1], send_sem=send2.at[d - 1], recv_sem=recv2.at[d - 1],
-            device_id=xy_device(d, core), device_id_type=MESH)
-        copy.start()
-        out2.append(copy)
+    for k, step in enumerate(STEPS):
+        pairs[k].wait_recv()
+        for d in [NY * step + dy for dy in (2, 1, 3, 0) if step or dy]:
+            qx, qy = xy_at(d)
+            there = qx * NY + qy
+            mine = NXY * core + there
+            y[mine] = y[mine] + r1[there]
+            copy = pltpu.make_async_remote_copy(
+                src_ref=y.at[mine], dst_ref=r2.at[d - 1], send_sem=send2.at[d - 1], recv_sem=recv2.at[d - 1],
+                device_id=xy_device(d, core), device_id_type=MESH)
+            copy.start()
+            out2.append(copy)
     total = y[NXY * core + xy] + r1[xy]
 
-    @pl.when(core == 1)
-    def _():
-        pl.semaphore_wait(barrier, 2 * (NZ - 1))
-        signal(line_here, sibling)
-
-    @pl.when(core == 0)
-    def _():
-        pl.semaphore_wait(line_here, 1)
-
-    for copy, d in zip(out2, FAR_XY):
+    for copy in out2:
         copy.wait_recv()
     for d in range(1, NXY):
         total = total + r2[d - 1]
@@ -169,6 +176,8 @@
             recv_sem=recv3.at[d - 1], device_id=z_device(d, core), device_id_type=MESH)
         copy.start()
         out3.append(copy)
+    for copy in pairs + out2:
+        copy.wait_send()
     for copy in out3:
         copy.wait_recv()
     scale = 1.0 / math.sqrt(131072)
@@ -197,6 +206,9 @@
             device_id=xy_device(d, core), device_id_type=MESH)
         out4[d].start()
 
+    for copy in out3:
+        copy.wait_send()
+
     wanted = 8 * px + 4 * zh + py
     holder = wanted // NXY == core
     where = wanted % NXY
@@ -248,7 +260,7 @@
         swaps.append((swap, step, came))
         at = pl.multiple_of(512 * core + 128 * came, 128)
         out_ref[:, :, pl.ds(at, 128)] = found[64:].reshape(4, 16, 128)
-    for copy in [pair] + out2 + out3 + list(out4.values()):
+    for copy in out4.values():
         copy.wait_send()
     for swap, step, came in swaps:
         swap.wait_recv()
@@ -284,7 +296,7 @@
             pltpu.VMEM((32, 256), jnp.bfloat16),
             pltpu.VMEM((4, 64, 128), jnp.float32),
             pltpu.VMEM((4, 64, 128), jnp.float32),
-            dma((11,)), dma, dma, dma((15,)), dma((15,)), dma((15,)), dma((15,)), dma((15,)), dma((15,)),
+            dma((11,)), dma((4,)), dma((4,)), dma((15,)), dma((15,)), dma((15,)), dma((15,)), dma((15,)), dma((15,)),
             dma, dma, dma((4,)), dma((4,)), pltpu.SemaphoreType.REGULAR, pltpu.SemaphoreType.REGULAR,
         ],
         compiler_params=pltpu.CompilerParams(

time: 39.6 us -> 38.8 us (0.980)
  Pallas kernels: 38.8 us -> 37.9 us
    pallas_call x1, Pallas kernels: 38.8 us -> 37.9 us  [body(): pl.pallas_call(kernel, out_shape=jax.ShapeDtypeStruct((4, 16, 1024), jnp....]
where the time goes in v5:
time: 38.8 us; the launch traced here: 38.7 us
  Pallas kernels  37.9 us (98%)
  local copies, waits for them, and re-layouts  0.71 us (2%)
    pallas_call x1, Pallas kernels, body(): pl.pallas_call(kernel, out_shape=jax.ShapeDtypeStruct((4, 16, 1024), jnp....  37.9 us

profile of v5, /device:TPU:1, one launch (start us, length us, event | category | flops | bytes accessed | tf_op | source)
XLA Modules:
  0.0 38.7 jit_solution(3482988183339984174)
XLA Ops:
  0.0 37.9 %shard_map.46 = f32[4,16,1024]{2,1,0:T(8,128)S(1)} custom-call(bf16[128,2048]{1,0:T(8,128)(2,1)} %x_hbm.1, s32[1,2048]{1,0:T(1,128)} %bitcast.3, s32[8,128]{1,0:T(8,128)} %bitcast.4, s32[1,128]{1,0:T(1,128)} %bitcast.5), custom_call_target="tpu_custom_call" | custom-call | tf_op jit(solution)/shard_map/pallas_call | solution.py:277
  37.9 0.7 %copy.6 = f32[4,16,1024]{2,1,0:T(8,128)} copy(f32[4,16,1024]{2,1,0:T(8,128)S(1)} %shard_map.46) | data formatting | bytes 524288

commit v6 on v5

--- a/solution.py
+++ b/solution.py
@@ -21,7 +21,7 @@
 
 def kernel(x_hbm, sg_hbm, col_hbm, lab_hbm, out_ref, x_ref, sg_ref, col_ref, lab_ref, xs, s, flip, y, r1, r2, fold, r3, g,
            rows32, give, take, load, send1, recv1, send2, recv2, send3, recv3, send4, recv4, send5, recv5, send6, recv6,
-           both_here, all_here):
+           both_here, all_here, line_here):
     loads = [pltpu.make_async_copy(*pair, load.at[i]) for i, pair in enumerate(
         [(col_hbm, col_ref), (sg_hbm, sg_ref), (lab_hbm, lab_ref)]
         + [(x_hbm.at[pl.ds(16 * k, 16)], x_ref.at[pl.ds(16 * k, 16)]) for k in range(8)])]
@@ -56,17 +56,21 @@
         pl.semaphore_signal(sem, inc=1, device_id=device, device_id_type=MESH)
 
     barrier = pltpu.get_barrier_semaphore()
-
-    @pl.when(core == 0)
+    hub = (px // 2) * (py // 2) == 1
+    hub_x, hub_y = 3 - (px + 1) // 2 % 2, 3 - (py + 1) // 2 % 2
+    plain = jnp.logical_not(hub)
+
+    @pl.when((core == 0) & plain | (core == 1) & hub)
     def _():
         signal(barrier, sibling)
 
-    for d in FAR_Z:
-        signal(barrier, z_device(d, 0))
     for d in FAR_XY:
         signal(barrier, xy_device(d, 0))
-
-    @pl.when(core == 1)
+    for d in FAR_Z:
+        other = (plane + d) % NZ
+        signal(barrier, {"feat": feat_of(hub_x, other // NG, hub_y, 1), "tok": other % NG})
+
+    @pl.when((core == 1) & plain)
     def _():
         pl.semaphore_wait(barrier, 1)
         signal(both_here, sibling)
@@ -105,9 +109,18 @@
 
     half_of(1 - core)
 
-    @pl.when(core == 0)
+    @pl.when((core == 0) & plain)
     def _():
         pl.semaphore_wait(both_here, 1)
+
+    @pl.when((core == 0) & hub)
+    def _():
+        pl.semaphore_wait(barrier, 2 * (NXY - 1) + 1)
+        signal(all_here, sibling)
+
+    @pl.when((core == 1) & hub)
+    def _():
+        pl.semaphore_wait(all_here, 1)
 
     pairs = []
     for k, step in enumerate(STEPS):
@@ -128,12 +141,12 @@
     spread = jnp.concatenate(
         [jnp.where(slot == within + 32.0 * q, 1.0, 0.0).astype(jnp.bfloat16) for q in range(NG)], axis=1)
 
-    @pl.when(core == 0)
-    def _():
-        pl.semaphore_wait(barrier, 2 * (NXY - 1) + 2 * (NZ - 1))
+    @pl.when((core == 0) & plain)
+    def _():
+        pl.semaphore_wait(barrier, 2 * (NXY - 1))
         signal(all_here, sibling)
 
-    @pl.when(core == 1)
+    @pl.when((core == 1) & plain)
     def _():
         pl.semaphore_wait(all_here, 1)
 
@@ -152,6 +165,15 @@
             out2.append(copy)
     total = y[NXY * core + xy] + r1[xy]
 
+
+    @pl.when((core == 1) & hub)
+    def _():
+        pl.semaphore_wait(barrier, 8 * (NZ - 1))
+        signal(line_here, sibling)
+        for qx, qy in ((3 - px, 3 - py), (3 - px, py), (px, 3 - py)):
+            for c in range(NC):
+                signal(line_here, {"feat": feat_of(qx, zh, qy, c), "tok": tok})
+
     for copy in out2:
         copy.wait_recv()
     for d in range(1, NXY):
@@ -169,6 +191,11 @@
         for k in range(1, 4):
             tile = jnp.where(quarter == k, picked[8 * k:8 * k + 8, 128 * q:128 * q + 128], tile)
         fold[q] = tile
+
+    @pl.when((core == 0) | plain)
+    def _():
+        pl.semaphore_wait(line_here, 1)
+
     out3 = []
     for d in FAR_Z:
         copy = pltpu.make_async_remote_copy(
@@ -298,6 +325,7 @@
             pltpu.VMEM((4, 64, 128), jnp.float32),
             dma((11,)), dma((4,)), dma((4,)), dma((15,)), dma((15,)), dma((15,)), dma((15,)), dma((15,)), dma((15,)),
             dma, dma, dma((4,)), dma((4,)), pltpu.SemaphoreType.REGULAR, pltpu.SemaphoreType.REGULAR,
+            pltpu.SemaphoreType.REGULAR,
         ],
         compiler_params=pltpu.CompilerParams(
             collective_id=0, has_side_effects=True, vmem_limit_bytes=40 * 1024 * 1024),

time: 38.8 us -> 38.6 us (level)
  no operation moved by 1% of the time
where the time goes in v6:
time: 38.6 us; the launch traced here: 38.4 us
  Pallas kernels  37.7 us (98%)
  local copies, waits for them, and re-layouts  0.71 us (2%)
    pallas_call x1, Pallas kernels, body(): pl.pallas_call(kernel, out_shape=jax.ShapeDtypeStruct((4, 16, 1024), jnp....  37.7 us

profile of v6, /device:TPU:1, one launch (start us, length us, event | category | flops | bytes accessed | tf_op | source)
XLA Modules:
  0.0 38.4 jit_solution(1492800234416052471)
XLA Ops:
  0.0 37.7 %shard_map.46 = f32[4,16,1024]{2,1,0:T(8,128)S(1)} custom-call(bf16[128,2048]{1,0:T(8,128)(2,1)} %x_hbm.1, s32[1,2048]{1,0:T(1,128)} %bitcast.3, s32[8,128]{1,0:T(8,128)} %bitcast.4, s32[1,128]{1,0:T(1,128)} %bitcast.5), custom_call_target="tpu_custom_call" | custom-call | tf_op jit(solution)/shard_map/pallas_call | solution.py:304
  37.7 0.7 %copy.6 = f32[4,16,1024]{2,1,0:T(8,128)} copy(f32[4,16,1024]{2,1,0:T(8,128)S(1)} %shard_map.46) | data formatting | bytes 524288

commit v7 on v6

--- a/solution.py
+++ b/solution.py
@@ -25,8 +25,6 @@
     loads = [pltpu.make_async_copy(*pair, load.at[i]) for i, pair in enumerate(
         [(col_hbm, col_ref), (sg_hbm, sg_ref), (lab_hbm, lab_ref)]
         + [(x_hbm.at[pl.ds(16 * k, 16)], x_ref.at[pl.ds(16 * k, 16)]) for k in range(8)])]
-    for copy in loads:
-        copy.start()
     f = lax.axis_index("feat")
     tok = lax.axis_index("tok")
     core = f % NC
@@ -60,12 +58,15 @@
     hub_x, hub_y = 3 - (px + 1) // 2 % 2, 3 - (py + 1) // 2 % 2
     plain = jnp.logical_not(hub)
 
-    @pl.when((core == 0) & plain | (core == 1) & hub)
-    def _():
-        signal(barrier, sibling)
-
     for d in FAR_XY:
         signal(barrier, xy_device(d, 0))
+
+    @pl.when((core == 0) & plain | (core == 1) & hub)
+    def _():
+        signal(barrier, sibling)
+
+    for copy in loads:
+        copy.start()
     for d in FAR_Z:
         other = (plane + d) % NZ
         signal(barrier, {"feat": feat_of(hub_x, other // NG, hub_y, 1), "tok": other % NG})
@@ -137,9 +138,14 @@
     earlier = jnp.where((row == col) & (lane < above), 1.0, 0.0)
     rank = jnp.sum(earlier, axis=1, keepdims=True)
     slot = col.astype(jnp.float32) * 8.0 + rank
-    within = (lane % 32).astype(jnp.float32)
+    at = lane.astype(jnp.float32)
     spread = jnp.concatenate(
-        [jnp.where(slot == within + 32.0 * q, 1.0, 0.0).astype(jnp.bfloat16) for q in range(NG)], axis=1)
+        [jnp.where(slot == at + 128.0 * q, 1.0, 0.0).astype(jnp.bfloat16) for q in range(2)], axis=1)
+
+    for copy in pairs:
+        copy.wait_recv()
+    own = pl.ds(NXY * core, NXY)
+    y[own] = y[own] + r1[...]
 
     @pl.when((core == 0) & plain)
     def _():
@@ -152,18 +158,16 @@
 
     out2 = []
     for k, step in enumerate(STEPS):
-        pairs[k].wait_recv()
         for d in [NY * step + dy for dy in (2, 1, 3, 0) if step or dy]:
             qx, qy = xy_at(d)
             there = qx * NY + qy
             mine = NXY * core + there
-            y[mine] = y[mine] + r1[there]
             copy = pltpu.make_async_remote_copy(
                 src_ref=y.at[mine], dst_ref=r2.at[d - 1], send_sem=send2.at[d - 1], recv_sem=recv2.at[d - 1],
                 device_id=xy_device(d, core), device_id_type=MESH)
             copy.start()
             out2.append(copy)
-    total = y[NXY * core + xy] + r1[xy]
+    total = y[NXY * core + xy]
 
 
     @pl.when((core == 1) & hub)
@@ -187,9 +191,12 @@
     picked = picked[0:32] + picked[32:64] + picked[64:96]
     quarter = lax.broadcasted_iota(jnp.int32, (8, 128), 1) // 32
     for q in range(NG):
-        tile = picked[0:8, 128 * q:128 * q + 128]
-        for k in range(1, 4):
-            tile = jnp.where(quarter == k, picked[8 * k:8 * k + 8, 128 * q:128 * q + 128], tile)
+        tile = None
+        for k in range(4):
+            part = picked[8 * k:8 * k + 8, 128 * (q // 4):128 * (q // 4) + 128]
+            if q % 4 != k:
+                part = pltpu.roll(part, (k - q % 4) % 4 * 32, 1)
+            tile = part if tile is None else jnp.where(quarter == k, part, tile)
         fold[q] = tile
 
     @pl.when((core == 0) | plain)
@@ -257,7 +264,6 @@
 
     @pl.when(holder)
     def _():
-        hand.wait_send()
         rows32[...] = g[where]
 
     @pl.when(jnp.logical_not(holder))
@@ -295,6 +301,10 @@
         out_ref[:, :, pl.ds(at, 128)] = take[step].reshape(4, 16, 128)
     for swap, step, came in swaps:
         swap.wait_send()
+
+    @pl.when(holder)
+    def _():
+        hand.wait_send()
 
 
 def body(features, signs, columns, labels):

time: 38.6 us -> 38.8 us (level)
  no operation moved by 1% of the time
where the time goes in v7:
time: 38.8 us; the launch traced here: 38.6 us
  Pallas kernels  37.9 us (98%)
  local copies, waits for them, and re-layouts  0.71 us (2%)
    pallas_call x1, Pallas kernels, body(): pl.pallas_call(kernel, out_shape=jax.ShapeDtypeStruct((4, 16, 1024), jnp....  37.9 us

profile of v7, /device:TPU:1, one launch (start us, length us, event | category | flops | bytes accessed | tf_op | source)
XLA Modules:
  0.0 38.6 jit_solution(6383157990102371254)
XLA Ops:
  0.0 37.9 %shard_map.46 = f32[4,16,1024]{2,1,0:T(8,128)S(1)} custom-call(bf16[128,2048]{1,0:T(8,128)(2,1)} %x_hbm.1, s32[1,2048]{1,0:T(1,128)} %bitcast.3, s32[8,128]{1,0:T(8,128)} %bitcast.4, s32[1,128]{1,0:T(1,128)} %bitcast.5), custom_call_target="tpu_custom_call" | custom-call | tf_op jit(solution)/shard_map/pallas_call | solution.py:314
  37.9 0.7 %copy.6 = f32[4,16,1024]{2,1,0:T(8,128)} copy(f32[4,16,1024]{2,1,0:T(8,128)S(1)} %shard_map.46) | data formatting | bytes 524288

commit v8 on v6

--- a/solution.py
+++ b/solution.py
@@ -81,20 +81,24 @@
     high = kept_at >> 11 & f
     for shift in (4, 2, 1):
         high = high ^ high >> shift
-    code = kept_at & 127 | (high & 1) << 7 | (kept_at & 1920) << 1
-    for i in range(8):
-        c = jnp.broadcast_to(code[i:i + 1, :], (128, 128)).T
-        v = c & (lane | 128)
-        for shift in (4, 2, 1):
-            v = v ^ v >> shift
-        parts = [(1 - 2 * (v & 1)).astype(jnp.float32).astype(jnp.bfloat16)]
-        for bit in range(3):
-            turn = (1 - 2 * (c >> 8 + bit & 1)).astype(jnp.float32).astype(jnp.bfloat16)
-            parts = parts + [part * turn for part in parts]
-        for block in range(8):
-            s[i, :, 128 * block:128 * block + 128] = parts[block]
-        flip[i] = (1 - 2 * (c >> 11 & 1)).astype(jnp.float32)
-
+    col_ref[...] = kept_at & 127 | (high & 1) << 7 | (kept_at & 1920) << 1
+
+    def signs_of(c):
+        for n in range(4):
+            i = 4 * c + n
+            code = jnp.broadcast_to(col_ref[pl.ds(i, 1), :], (128, 128)).T
+            v = code & (lane | 128)
+            for shift in (4, 2, 1):
+                v = v ^ v >> shift
+            parts = [(1 - 2 * (v & 1)).astype(jnp.float32).astype(jnp.bfloat16)]
+            for bit in range(3):
+                turn = (1 - 2 * (code >> 8 + bit & 1)).astype(jnp.float32).astype(jnp.bfloat16)
+                parts = parts + [part * turn for part in parts]
+            for block in range(8):
+                s[i, :, 128 * block:128 * block + 128] = parts[block]
+            flip[i] = (1 - 2 * (code >> 11 & 1)).astype(jnp.float32)
+
+    signs_of(1 - core)
     for copy in loads[1:]:
         copy.wait()
     sign = sg_ref[...].astype(jnp.float32).astype(jnp.bfloat16)
@@ -129,6 +133,7 @@
             src_ref=y.at[pl.ds(NXY * (1 - core) + there, 4)], dst_ref=r1.at[pl.ds(there, 4)],
             send_sem=send1.at[k], recv_sem=recv1.at[k], device_id=sibling, device_id_type=MESH))
         pairs[k].start()
+    signs_of(core)
     half_of(core)
 
     row = jnp.broadcast_to(lab_ref[...], (128, 128))

time: 38.6 us -> 38.6 us (level)
  no operation moved by 1% of the time
where the time goes in v8:
time: 38.6 us; the launch traced here: 38.4 us
  Pallas kernels  37.7 us (98%)
  local copies, waits for them, and re-layouts  0.71 us (2%)
    pallas_call x1, Pallas kernels, body(): pl.pallas_call(kernel, out_shape=jax.ShapeDtypeStruct((4, 16, 1024), jnp....  37.7 us

profile of v8, /device:TPU:1, one launch (start us, length us, event | category | flops | bytes accessed | tf_op | source)
XLA Modules:
  0.0 38.4 jit_solution(6001116322418142595)
XLA Ops:
  0.0 37.7 %shard_map.46 = f32[4,16,1024]{2,1,0:T(8,128)S(1)} custom-call(bf16[128,2048]{1,0:T(8,128)(2,1)} %x_hbm.1, s32[1,2048]{1,0:T(1,128)} %bitcast.3, s32[8,128]{1,0:T(8,128)} %bitcast.4, s32[1,128]{1,0:T(1,128)} %bitcast.5), custom_call_target="tpu_custom_call" | custom-call | tf_op jit(solution)/shard_map/pallas_call | solution.py:309
  37.7 0.7 %copy.6 = f32[4,16,1024]{2,1,0:T(8,128)} copy(f32[4,16,1024]{2,1,0:T(8,128)S(1)} %shard_map.46) | data formatting | bytes 524288
